TPU v7x, 256 devices: a whole 4x4x8 slice. The times are simulated.
256 devices in a mesh: stream: 2 (over z_hi), dp: 16 (over x, y), tensor: 8 (over z_lo, core).
Axes of the slice: x: 4, y: 4, z: 8 (z_hi: 2, z_lo: 4; z = z_hi * 4 + z_lo), core: 2. Of those that a mesh axis runs over, the one named last changes fastest.
Arguments:
- hidden: bfloat16 [2, 256, 8192], P('stream', 'tensor', 'dp'), may hold values from -3 to 3
- cached_rotated_keys: bfloat16 [2, 256, 8, 256, 128], P('stream', 'dp', 'tensor'), may hold values from -6 to 6
- cached_values: bfloat16 [2, 256, 8, 256, 128], P('stream', 'dp', 'tensor'), may hold values from -18 to 18
- cache_lengths: int32 [2, 256], P('stream', 'dp'), may hold values from 1 to 256, as said below
- recent_ids: int32 [256, 128], replicated, may hold values from 0 to 65535
- guidance: float32 [256], replicated, may hold values from 1 to 3
- w_query: bfloat16 [8192, 8192], P('dp', 'tensor'), may hold values from -0.0625 to 0.0625
- key_value_weight: bfloat16 [8192, 2, 1024], P('dp', None, 'tensor'), may hold values from -0.0625 to 0.0625
- w_output: bfloat16 [8192, 8192], P('tensor', 'dp'), may hold values from -0.0625 to 0.0625
- norm_gain: bfloat16 [8192], P('dp'), may hold values from 0.5 to 1.5
- w_head: bfloat16 [8192, 65536], P(None, ('dp', 'tensor')), may hold values from -0.16503906 to 0.16503906
Outputs:
- guided_logprobs: float32 [256, 65536], P('stream', ('dp', 'tensor'))
Inputs may be any that keep to these rules, and one draw needn't show every extreme that they name: `cache_lengths`: every prompt has 1 to 256 filled slots in each stream; some prompt has all 256; lengths differ widely from one group of 16 prompts to the next.
All inputs are finite; a program needn't handle non-finite values.
Results may differ from a plain program's by a relative error of at most 0.0025.
Values may be sent and summed in bfloat16 or wider, within the bound.
A program may use at most 64 MiB of HBM per device.

v0:
```python
import jax
import jax.numpy as jnp
from jax import lax
from jax.sharding import PartitionSpec as P

MODEL_WIDTH = 8192
HEAD_SIZE = 128
rope_theta = 500000.0
penalty_step = 1.5
norm_eps = 1e-05


def partner_2(value, axis, distance):
    mask = 2**distance
    pairs = [(source, source ^ mask) for source in range(lax.axis_size(axis))]
    return lax.ppermute(value, axis, pairs)


def rotate(values, positions):
    halfway = values.shape[-1] // 2
    frequency = rope_theta ** (-(jnp.arange(halfway, dtype=jnp.float32) * 2.0 / values.shape[-1]))
    angles = positions.astype(jnp.float32)[:, None, None] * frequency
    cosine_term = jnp.cos(angles)
    sine_term = jnp.sin(angles)
    first_half = values[..., :halfway]
    second_half = values[..., halfway:]
    return jnp.concatenate(
        [
            first_half * cosine_term - second_half * sine_term,
            second_half * cosine_term + first_half * sine_term,
        ],
        axis=-1,
    )


def repeat_counts(recent_ids, first_column, width):
    columns = first_column + jnp.arange(width, dtype=jnp.int32)
    return jnp.sum((recent_ids[:, :, None] == columns[None, None, :]).astype(jnp.float32), 1)


def body(
    hidden,
    cached_rotated_keys,
    cached_values,
    cache_lengths,
    recent_ids,
    guidance,
    w_query,
    key_value_weight,
    w_output,
    norm_gain,
    w_head,
):
    local_width = hidden.shape[2]
    query_cols = w_query.shape[1]
    kv_cols = key_value_weight.shape[2]
    local_prompts = cache_lengths.shape[1]
    lengths = cache_lengths[0]
    vocab_local = w_head.shape[1]
    all_rows = lax.all_gather(hidden[0], "tensor", axis=0, tiled=True)
    kv_flat = key_value_weight.reshape(local_width, 2 * kv_cols)
    projected = lax.psum_scatter(
        jnp.concatenate(
            [
                jnp.dot(all_rows, w_query, preferred_element_type=jnp.float32),
                jnp.dot(all_rows, kv_flat, preferred_element_type=jnp.float32),
            ],
            axis=1,
        ),
        "dp",
        scatter_dimension=0,
        tiled=True,
    )
    query_heads = query_cols // HEAD_SIZE
    kv_heads = kv_cols // HEAD_SIZE
    rotated_query = rotate(
        projected[:, :query_cols].reshape(local_prompts, query_heads, HEAD_SIZE), lengths
    ).astype(jnp.bfloat16)
    key_value_rows = projected[:, query_cols:].reshape(local_prompts, 2, kv_heads, HEAD_SIZE)
    fresh_key = rotate(key_value_rows[:, 0], lengths).astype(jnp.bfloat16)
    value_new = key_value_rows[:, 1].astype(jnp.bfloat16)
    grouped_queries = rotated_query.reshape(
        local_prompts, kv_heads, query_heads // kv_heads, HEAD_SIZE
    )
    attention_scale = HEAD_SIZE ** (-0.5)
    key_block = cached_rotated_keys[0]
    value_block = cached_values[0]
    scores = (
        jnp.einsum(
            "pkgd,pksd->pkgs", grouped_queries, key_block, preferred_element_type=jnp.float32
        )
        * attention_scale
    )
    self_score = (
        jnp.einsum("pkgd,pkd->pkg", grouped_queries, fresh_key, preferred_element_type=jnp.float32)
        * attention_scale
    )
    valid = jnp.arange(key_block.shape[2], dtype=jnp.int32)[None, :] < lengths[:, None]
    exps = jnp.where(valid[:, None, None, :], jnp.exp(scores), 0.0)
    own_exp = jnp.exp(self_score)
    denominator = jnp.sum(exps, -1) + own_exp
    weights = (exps / denominator[..., None]).astype(jnp.bfloat16)
    own_weight = (own_exp / denominator).astype(jnp.bfloat16)
    attended = jnp.einsum(
        "pkgs,pksd->pkgd", weights, value_block, preferred_element_type=jnp.float32
    )
    attended = (
        attended
        + own_weight.astype(jnp.float32)[..., None] * value_new.astype(jnp.float32)[:, :, None, :]
    )
    attended = attended.reshape(local_prompts, query_cols).astype(jnp.bfloat16)
    partial_out = jnp.dot(
        lax.all_gather(attended, "dp", axis=0, tiled=True),
        w_output,
        preferred_element_type=jnp.float32,
    )
    output_sum = lax.psum_scatter(partial_out, "tensor", scatter_dimension=0, tiled=True)
    residual = (hidden[0].astype(jnp.float32) + output_sum).astype(jnp.bfloat16)
    widened = residual.astype(jnp.float32)
    squares = lax.psum(jnp.sum(widened * widened, 1), "dp")
    inverse = lax.rsqrt(squares / MODEL_WIDTH + norm_eps)
    normed = (widened * inverse[:, None] * norm_gain.astype(jnp.float32)).astype(jnp.bfloat16)
    normed_all = lax.all_gather(normed, "tensor", axis=0, tiled=True)
    logits = jnp.dot(
        lax.all_gather(normed_all, "dp", axis=1, tiled=True),
        w_head,
        preferred_element_type=jnp.float32,
    )
    stream_side = lax.axis_index("stream")
    half_rows = logits.shape[0] // 2
    mine_start = stream_side * half_rows
    other_start = (1 - stream_side) * half_rows
    column_base = lax.axis_index(("dp", "tensor")) * vocab_local
    mine = lax.dynamic_slice_in_dim(logits, mine_start, half_rows, 0)
    sending = lax.dynamic_slice_in_dim(logits, other_start, half_rows, 0)
    partner = partner_2(sending, "stream", 0)
    conditional = jnp.where(stream_side == 0, mine, partner)
    unconditional = jnp.where(stream_side == 0, partner, mine)
    guide = lax.dynamic_slice_in_dim(guidance, mine_start, half_rows, 0)[:, None]
    recent_mine = lax.dynamic_slice_in_dim(recent_ids, mine_start, half_rows, 0)
    guided = unconditional + guide * (conditional - unconditional)
    guided = guided - penalty_step * repeat_counts(recent_mine, column_base, vocab_local)
    totals = lax.psum(jnp.sum(jnp.exp(guided), 1), ("dp", "tensor"))
    return guided - jnp.log(totals)[:, None]


def solution(mesh):
    return jax.shard_map(
        body,
        mesh=mesh,
        in_specs=(
            P("stream", "tensor", "dp"),
            P("stream", "dp", "tensor", None, None),
            P("stream", "dp", "tensor", None, None),
            P("stream", "dp"),
            P(),
            P(),
            P("dp", "tensor"),
            P("dp", None, "tensor"),
            P("tensor", "dp"),
            P("dp"),
            P(None, ("dp", "tensor")),
        ),
        out_specs=P("stream", ("dp", "tensor")),
        check_vma=False,
    )
```

profile of v0, /device:TPU:128, one launch (start us, length us, event | category | flops | bytes accessed | tf_op | source)
XLA Modules:
  0.0 647.4 jit_solution(1154850240006349418)
XLA Ops:
  6.5 0.0 copy-start
  6.5 0.0 copy-start.3
  6.5 0.0 copy-start.1
  6.5 0.0 copy-start.2
  6.5 0.0 copy-start.5
  6.5 0.0 copy-start.6
  6.6 0.0 copy-start.4
  6.6 0.0 reduce-scatter.3.cloned.1.call-start
  6.6 14.5 %all-gather = bf16[1,256,512]{2,1,0:T(8,128)(2,1)S(1)} all-gather(bf16[1,32,512]{2,1,0:T(8,128)(2,1)} %param.11), channel_id=2, replica_groups=mesh['stream'=2,'dp'=16,'tensor'=8] {'tensor'}, dimensions={1}, use_global_device_ids=true | all-gather | bytes 294912 | tf_op jit(solution)/shard_map/all_gather | solution.py:60
  21.1 0.0 copy-done
  21.1 0.5 fusion.9
  21.6 1.2 fusion.5
  22.8 1.2 pad_maximum_fusion
  24.0 0.0 reduce-scatter.3.cloned.1.call-update
  24.0 0.0 reduce-scatter.5.cloned.1.call-start
  24.1 0.7 bitcast_convert_fusion
  24.7 0.7 iota_compare_fusion
  25.4 0.1 multiply_cosine_fusion.1
  25.6 79.2 %reduce-scatter.3.cloned.1.call-done = f32[16,1280]{1,0:T(8,128)} async-done(((f32[256,1280]{1,0:T(8,128)}), f32[16,1280]{1,0:T(8,128)}) %reduce-scatter.3.cloned.1.call-update) | async-done | bytes 81936 | tf_op jit(solution)/shard_map/reduce_scatter | solution.py:62
  104.8 0.7 slice.36
  105.6 0.1 fusion.30
  105.7 0.8 slice_bitcast_fusion
  106.6 0.1 maximum_bitcast_fusion
  106.6 0.1 subtract_convert_fusion
  106.7 0.2 fusion.25
  106.9 1.7 fusion.33
  108.7 0.0 copy-done.1
  108.7 0.3 fusion.2
  109.0 23.3 %all_gather.13 = bf16[256,1024]{1,0:T(8,128)(2,1)S(1)} all-gather(bf16[16,1024]{1,0:T(8,128)(2,1)S(1)} %bitcast.51), channel_id=1, replica_groups=mesh['stream'=2,'dp'=16,'tensor'=8] {'dp'}, dimensions={0}, use_global_device_ids=true | all-gather | bytes 557056 | tf_op jit(solution)/shard_map/all_gather | solution.py:113
  132.3 0.0 copy-done.2
  132.3 1.2 fusion.34
  133.5 0.0 reduce-scatter.5.cloned.1.call-update
  133.6 0.0 all-gather.3.cloned.1.call-start
  133.6 0.0 copy-done.5
  133.6 32.9 %reduce-scatter.5.cloned.1.call-done = f32[32,512]{1,0:T(8,128)} async-done(((f32[256,512]{1,0:T(8,128)}), f32[32,512]{1,0:T(8,128)}) %reduce-scatter.5.cloned.1.call-update) | async-done | bytes 65552 | tf_op jit(solution)/shard_map/reduce_scatter | solution.py:117
  166.5 0.0 copy-done.3
  166.5 1.0 fusion.11
  167.5 40.3 %psum.14 = f32[32]{0:T(128)S(1)} all-reduce(f32[32]{0:T(128)S(1)} %fusion.11), channel_id=1, replica_groups=mesh['stream'=2,'dp'=16,'tensor'=8] {'dp'}, use_global_device_ids=true, to_apply=%region_4.5 | all-reduce | flops 32 | bytes 256 | tf_op jit(solution)/shard_map/psum | solution.py:120
  207.8 0.9 fusion.13
  208.7 15.3 %all_gather.14 = bf16[256,512]{1,0:T(8,128)(2,1)} all-gather(bf16[32,512]{1,0:T(8,128)(2,1)S(1)} %fusion.13), channel_id=1, replica_groups=mesh['stream'=2,'dp'=16,'tensor'=8] {'tensor'}, dimensions={0}, use_global_device_ids=true | all-gather | bytes 294912 | tf_op jit(solution)/shard_map/all_gather | solution.py:123
  224.0 0.0 all-gather.3.cloned.1.call-update
  224.1 0.0 copy-done.6
  224.1 0.1 dynamic_slice.14
  224.2 0.0 copy-done.4
  224.2 58.3 %all-gather.3.cloned.1.call-done = bf16[256,8192]{1,0:T(8,128)(2,1)} async-done(((bf16[256,512]{1,0:T(8,128)(2,1)}), bf16[256,8192]{1,0:T(8,128)(2,1)}) %all-gather.3.cloned.1.call-update) | async-done | bytes 4194320 | tf_op jit(solution)/shard_map/all_gather | solution.py:125
  282.5 7.0 %fusion.35 = f32[256,512]{1,0:T(8,128)S(1)} fusion(bf16[256,8192]{1,0:T(8,128)(2,1)} %all-gather.3.cloned.1.call-done, bf16[8192,512]{1,0:T(8,128)(2,1)} %param.21), kind=kOutput, calls=%fused_computation.66 | convolution fusion | flops 2147483648 | bytes 13107200 | tf_op jit(solution)/shard_map/dot_general | solution.py:124
  289.5 0.3 collective-permute-start
  289.8 4.7 convert_reduce_fusion
  294.4 11.4 %collective-permute-done = f32[128,512]{1,0:T(8,128)S(1)} collective-permute-done((f32[128,512]{1,0:T(8,128)S(1)}, f32[128,512]{1,0:T(8,128)S(1)}, u32[]{:S(2)}, u32[]{:S(2)}) %collective-permute-start) | collective-permute-done | bytes 262176 | tf_op jit(solution)/shard_map/ppermute | solution.py:16
  305.8 0.2 exponential_reduce_fusion
  306.0 334.1 %psum.15 = f32[128]{0:T(128)S(1)} all-reduce(f32[128]{0:T(128)S(1)} %get-tuple-element.5), channel_id=1, replica_groups=mesh['stream'=2,'dp'=16,'tensor'=8] {'dp','tensor'}, use_global_device_ids=true, to_apply=%region_7.8 | all-reduce | flops 128 | bytes 1024 | tf_op jit(solution)/shard_map/psum | solution.py:143
  640.1 0.8 broadcast_subtract_fusion
  (13 shorter events, 0.1 us)
Async XLA Ops:
  6.5 14.6 %copy-start = (bf16[512,1024]{1,0:T(8,128)(2,1)S(1)}, bf16[512,1024]{1,0:T(8,128)(2,1)}, u32[]{:S(2)}) copy-start(bf16[512,1024]{1,0:T(8,128)(2,1)} %param.17) | copy-start | bytes 3145732
  6.5 160.0 %copy-start.3 = (bf16[1,32,512]{2,1,0:T(8,128)(2,1)S(1)}, bf16[1,32,512]{2,1,0:T(8,128)(2,1)}, u32[]{:S(2)}) copy-start(bf16[1,32,512]{2,1,0:T(8,128)(2,1)} %param.11) | copy-start | bytes 98308
  6.5 102.2 %copy-start.1 = (bf16[1,16,1,256,128]{4,3,2,1,0:T(8,128)(2,1)S(1)}, bf16[1,16,1,256,128]{4,3,2,1,0:T(8,128)(2,1)}, u32[]{:S(2)}) copy-start(bf16[1,16,1,256,128]{4,3,2,1,0:T(8,128)(2,1)} %param.13) | copy-start | bytes 3145732
  6.5 125.8 %copy-start.2 = (bf16[1024,512]{1,0:T(8,128)(2,1)S(1)}, bf16[1024,512]{1,0:T(8,128)(2,1)}, u32[]{:S(2)}) copy-start(bf16[1024,512]{1,0:T(8,128)(2,1)} %param.19) | copy-start | bytes 3145732
  6.5 127.1 %copy-start.5 = (bf16[512]{0:T(512)(128)(2,1)S(1)}, bf16[512]{0:T(512)(128)(2,1)}, u32[]{:S(2)}) copy-start(bf16[512]{0:T(512)(128)(2,1)} %param.20) | copy-start | bytes 3076
  6.5 217.5 %copy-start.6 = (f32[256]{0:T(256)S(1)}, f32[256]{0:T(256)}, u32[]{:S(2)}) copy-start(f32[256]{0:T(256)} %param.16) | copy-start | bytes 3076
  6.6 217.6 %copy-start.4 = (s32[256,128]{1,0:T(8,128)S(1)}, s32[256,128]{1,0:T(8,128)}, u32[]{:S(2)}) copy-start(s32[256,128]{1,0:T(8,128)} %param.15) | copy-start | bytes 393220
  6.6 98.2 %reduce-scatter.3.cloned.1.call-start = ((), (), s32[]{:S(2)}) async-start(), calls=%async_computation.2 | async-start | bytes 1392640 | tf_op jit(solution)/shard_map/reduce_scatter | solution.py:62
  24.0 142.5 %reduce-scatter.5.cloned.1.call-start = ((), (), s32[]{:S(2)}) async-start(), calls=%async_computation.3 | async-start | bytes 589824 | tf_op jit(solution)/shard_map/reduce_scatter | solution.py:117
  133.6 148.9 %all-gather.3.cloned.1.call-start = ((), (), s32[]{:S(2)}) async-start(), calls=%async_computation.4 | async-start | bytes 4456448 | tf_op jit(solution)/shard_map/all_gather | solution.py:125
  289.5 16.3 %collective-permute-start = (f32[128,512]{1,0:T(8,128)S(1)}, f32[128,512]{1,0:T(8,128)S(1)}, u32[]{:S(2)}, u32[]{:S(2)}) collective-permute-start(f32[128,512]{1,0:T(8,128)S(1)} %constant_dynamic-slice_fusion.1), channel_id=1, source_target_pairs={{0,128},{128,0},{1,129},{129,1},{2,130},{130,2},{3,131},{131,3},{4... | collective-permute-start | bytes 786440 | tf_op jit(solution)/shard_map/ppermute | solution.py:16
Sparse Core Ops, SparseCore 0:
  24.1 80.6 reduce-scatter.2
  133.7 32.7 reduce-scatter.4
  224.2 58.2 all-gather.2
where the time goes:
time: 648 us; the launch traced here: 647 us
  blocking collectives  427 us (66%)
  waiting for transfers between devices  182 us (28%)
  between operations  13.3 us (2%)
  matrix products  12.1 us (2%)
  other arithmetic  10.5 us (2%)
    psum x1, blocking collectives, body(): totals = lax.psum(jnp.sum(jnp.exp(guided), 1), ('dp', 'tensor'))  334 us
    reduce_scatter x1, waiting for transfers between devices, body(): lax.psum_scatter(jnp.concatenate([jnp.dot(all_rows, w_query, preferred_el...  79.2 us
    all_gather x1, waiting for transfers between devices, body(): lax.all_gather(normed_all, 'dp', axis=1, tiled=True)  58.3 us
    psum x1, blocking collectives, body(): squares = lax.psum(jnp.sum(widened * widened, 1), 'dp')  40.3 us
    reduce_scatter x1, waiting for transfers between devices, body(): lax.psum_scatter(partial_out, 'tensor', scatter_dimension=0, tiled=True)  32.9 us
    all_gather x1, blocking collectives, body(): lax.all_gather(attended, 'dp', axis=0, tiled=True)  23.3 us
    all_gather x1, blocking collectives, body(): normed_all = lax.all_gather(normed, 'tensor', axis=0, tiled=True)  15.3 us
    all_gather x1, blocking collectives, body(): all_rows = lax.all_gather(hidden[0], 'tensor', axis=0, tiled=True)  14.5 us
  transfers between devices with their start and end apart: 4, of which 4 were waited for; matrix products, arithmetic and copies ran while one was open for 1% of the time, Pallas kernels for 0%

commit v1 on v0

--- a/solution.py
+++ b/solution.py
@@ -2,6 +2,7 @@
 import jax.numpy as jnp
 from jax import lax
 from jax.sharding import PartitionSpec as P
+from jax.lax import psum
 
 MODEL_WIDTH = 8192
 HEAD_SIZE = 128
@@ -140,7 +141,8 @@
     recent_mine = lax.dynamic_slice_in_dim(recent_ids, mine_start, half_rows, 0)
     guided = unconditional + guide * (conditional - unconditional)
     guided = guided - penalty_step * repeat_counts(recent_mine, column_base, vocab_local)
-    totals = lax.psum(jnp.sum(jnp.exp(guided), 1), ("dp", "tensor"))
+    field_in = jnp.sum(jnp.exp(guided), 1)
+    totals = psum(psum(field_in, axis_name="tensor"), axis_name="dp")
     return guided - jnp.log(totals)[:, None]
 
 

time: 648 us -> 365 us (0.56)
  blocking collectives: 427 us -> 145 us
    psum x1 -> x2, blocking collectives: 334 us -> 51.7 us  [body(): totals = psum(psum(field_in, axis_name='tensor'), axis_name='dp')]
  transfers between devices with their start and end apart: 4 -> 4, of which waited for: 4 -> 4; matrix products, arithmetic and copies ran while one was open for 1% -> 2% of each run, Pallas kernels for 0% -> 0%
where the time goes in v1:
time: 365 us
  waiting for transfers between devices  182 us (50%)
  blocking collectives  145 us (40%)
  between operations  13.3 us (4%)
  matrix products  12.1 us (3%)
  other arithmetic  10.5 us (3%)
    reduce_scatter x1, waiting for transfers between devices, body(): lax.psum_scatter(jnp.concatenate([jnp.dot(all_rows, w_query, preferred_el...  79.2 us
    all_gather x1, waiting for transfers between devices, body(): lax.all_gather(normed_all, 'dp', axis=1, tiled=True)  58.3 us
    psum x2, blocking collectives, body(): totals = psum(psum(field_in, axis_name='tensor'), axis_name='dp')  51.7 us
    psum x1, blocking collectives, body(): squares = lax.psum(jnp.sum(widened * widened, 1), 'dp')  40.3 us
    reduce_scatter x1, waiting for transfers between devices, body(): lax.psum_scatter(partial_out, 'tensor', scatter_dimension=0, tiled=True)  32.9 us
    all_gather x1, blocking collectives, body(): lax.all_gather(attended, 'dp', axis=0, tiled=True)  23.3 us
    all_gather x1, blocking collectives, body(): normed_all = lax.all_gather(normed, 'tensor', axis=0, tiled=True)  15.3 us
    all_gather x1, blocking collectives, body(): all_rows = lax.all_gather(hidden[0], 'tensor', axis=0, tiled=True)  14.5 us
  transfers between devices with their start and end apart: 4, of which 4 were waited for; matrix products, arithmetic and copies ran while one was open for 2% of the time, Pallas kernels for 0%

profile of v1, /device:TPU:128, one launch (start us, length us, event | category | flops | bytes accessed | tf_op | source)
XLA Modules:
  0.0 365.1 jit_solution(7004600347445081312)
XLA Ops:
  6.5 0.0 copy-start
  6.5 0.0 copy-start.3
  6.5 0.0 copy-start.1
  6.5 0.0 copy-start.2
  6.5 0.0 copy-start.5
  6.5 0.0 copy-start.6
  6.6 0.0 copy-start.4
  6.6 0.0 reduce-scatter.3.cloned.1.call-start
  6.6 14.5 %all-gather = bf16[1,256,512]{2,1,0:T(8,128)(2,1)S(1)} all-gather(bf16[1,32,512]{2,1,0:T(8,128)(2,1)} %param.11), channel_id=2, replica_groups=mesh['stream'=2,'dp'=16,'tensor'=8] {'tensor'}, dimensions={1}, use_global_device_ids=true | all-gather | bytes 294912 | tf_op jit(solution)/shard_map/all_gather | solution.py:61
  21.1 0.0 copy-done
  21.1 0.5 fusion.9
  21.6 1.2 fusion.5
  22.8 1.2 pad_maximum_fusion
  24.0 0.0 reduce-scatter.3.cloned.1.call-update
  24.0 0.0 reduce-scatter.5.cloned.1.call-start
  24.1 0.7 bitcast_convert_fusion
  24.7 0.7 iota_compare_fusion
  25.4 0.1 multiply_cosine_fusion.1
  25.6 79.2 %reduce-scatter.3.cloned.1.call-done = f32[16,1280]{1,0:T(8,128)} async-done(((f32[256,1280]{1,0:T(8,128)}), f32[16,1280]{1,0:T(8,128)}) %reduce-scatter.3.cloned.1.call-update) | async-done | bytes 81936 | tf_op jit(solution)/shard_map/reduce_scatter | solution.py:63
  104.8 0.7 slice.36
  105.6 0.1 fusion.30
  105.7 0.8 slice_bitcast_fusion
  106.6 0.1 maximum_bitcast_fusion
  106.6 0.1 subtract_convert_fusion
  106.7 0.2 fusion.25
  106.9 1.7 fusion.33
  108.7 0.0 copy-done.1
  108.7 0.3 fusion.2
  109.0 23.3 %all_gather.13 = bf16[256,1024]{1,0:T(8,128)(2,1)S(1)} all-gather(bf16[16,1024]{1,0:T(8,128)(2,1)S(1)} %bitcast.51), channel_id=1, replica_groups=mesh['stream'=2,'dp'=16,'tensor'=8] {'dp'}, dimensions={0}, use_global_device_ids=true | all-gather | bytes 557056 | tf_op jit(solution)/shard_map/all_gather | solution.py:114
  132.3 0.0 copy-done.2
  132.3 1.2 fusion.34
  133.5 0.0 reduce-scatter.5.cloned.1.call-update
  133.6 0.0 all-gather.3.cloned.1.call-start
  133.6 0.0 copy-done.5
  133.6 32.9 %reduce-scatter.5.cloned.1.call-done = f32[32,512]{1,0:T(8,128)} async-done(((f32[256,512]{1,0:T(8,128)}), f32[32,512]{1,0:T(8,128)}) %reduce-scatter.5.cloned.1.call-update) | async-done | bytes 65552 | tf_op jit(solution)/shard_map/reduce_scatter | solution.py:118
  166.5 0.0 copy-done.3
  166.5 1.0 fusion.11
  167.5 40.3 %psum.21 = f32[32]{0:T(128)S(1)} all-reduce(f32[32]{0:T(128)S(1)} %fusion.11), channel_id=1, replica_groups=mesh['stream'=2,'dp'=16,'tensor'=8] {'dp'}, use_global_device_ids=true, to_apply=%region_4.5 | all-reduce | flops 32 | bytes 256 | tf_op jit(solution)/shard_map/psum | solution.py:121
  207.8 0.9 fusion.13
  208.7 15.3 %all_gather.14 = bf16[256,512]{1,0:T(8,128)(2,1)} all-gather(bf16[32,512]{1,0:T(8,128)(2,1)S(1)} %fusion.13), channel_id=1, replica_groups=mesh['stream'=2,'dp'=16,'tensor'=8] {'tensor'}, dimensions={0}, use_global_device_ids=true | all-gather | bytes 294912 | tf_op jit(solution)/shard_map/all_gather | solution.py:124
  224.0 0.0 all-gather.3.cloned.1.call-update
  224.1 0.0 copy-done.6
  224.1 0.1 dynamic_slice.14
  224.2 0.0 copy-done.4
  224.2 58.3 %all-gather.3.cloned.1.call-done = bf16[256,8192]{1,0:T(8,128)(2,1)} async-done(((bf16[256,512]{1,0:T(8,128)(2,1)}), bf16[256,8192]{1,0:T(8,128)(2,1)}) %all-gather.3.cloned.1.call-update) | async-done | bytes 4194320 | tf_op jit(solution)/shard_map/all_gather | solution.py:126
  282.5 7.0 %fusion.35 = f32[256,512]{1,0:T(8,128)S(1)} fusion(bf16[256,8192]{1,0:T(8,128)(2,1)} %all-gather.3.cloned.1.call-done, bf16[8192,512]{1,0:T(8,128)(2,1)} %param.21), kind=kOutput, calls=%fused_computation.66 | convolution fusion | flops 2147483648 | bytes 13107200 | tf_op jit(solution)/shard_map/dot_general | solution.py:125
  289.5 0.3 collective-permute-start
  289.8 4.7 %convert_reduce_fusion = f32[128,512]{1,0:T(8,128)S(1)} fusion(s32[512]{0:T(512)S(1)} %iota_add_fusion, s32[128,128]{1,0:T(8,128)S(1)} %constant_dynamic-slice_fusion), kind=kLoop, calls=%fused_computation | loop fusion | flops 25100288 | bytes 329728 | tf_op jit(solution)/shard_map/reduce_sum | solution.py:39
  294.4 11.4 %collective-permute-done = f32[128,512]{1,0:T(8,128)S(1)} collective-permute-done((f32[128,512]{1,0:T(8,128)S(1)}, f32[128,512]{1,0:T(8,128)S(1)}, u32[]{:S(2)}, u32[]{:S(2)}) %collective-permute-start) | collective-permute-done | bytes 262176 | tf_op jit(solution)/shard_map/ppermute | solution.py:17
  305.8 0.2 exponential_reduce_fusion
  306.0 13.6 %psum.22 = f32[128]{0:T(128)S(1)} all-reduce(f32[128]{0:T(128)S(1)} %get-tuple-element.5), channel_id=1, replica_groups=mesh['stream'=2,'dp'=16,'tensor'=8] {'tensor'}, use_global_device_ids=true, to_apply=%region_7.8 | all-reduce | flops 128 | bytes 1024 | tf_op jit(solution)/shard_map/psum | solution.py:145
  319.6 38.1 %psum.23 = f32[128]{0:T(128)S(1)} all-reduce(f32[128]{0:T(128)S(1)} %psum.22), channel_id=1, replica_groups=mesh['stream'=2,'dp'=16,'tensor'=8] {'dp'}, use_global_device_ids=true, to_apply=%region_8.9 | all-reduce | flops 128 | bytes 1024 | tf_op jit(solution)/shard_map/psum | solution.py:145
  357.7 0.8 broadcast_subtract_fusion
  (13 shorter events, 0.1 us)
Async XLA Ops:
  6.5 14.6 %copy-start = (bf16[512,1024]{1,0:T(8,128)(2,1)S(1)}, bf16[512,1024]{1,0:T(8,128)(2,1)}, u32[]{:S(2)}) copy-start(bf16[512,1024]{1,0:T(8,128)(2,1)} %param.17) | copy-start | bytes 3145732
  6.5 160.0 %copy-start.3 = (bf16[1,32,512]{2,1,0:T(8,128)(2,1)S(1)}, bf16[1,32,512]{2,1,0:T(8,128)(2,1)}, u32[]{:S(2)}) copy-start(bf16[1,32,512]{2,1,0:T(8,128)(2,1)} %param.11) | copy-start | bytes 98308
  6.5 102.2 %copy-start.1 = (bf16[1,16,1,256,128]{4,3,2,1,0:T(8,128)(2,1)S(1)}, bf16[1,16,1,256,128]{4,3,2,1,0:T(8,128)(2,1)}, u32[]{:S(2)}) copy-start(bf16[1,16,1,256,128]{4,3,2,1,0:T(8,128)(2,1)} %param.13) | copy-start | bytes 3145732
  6.5 125.8 %copy-start.2 = (bf16[1024,512]{1,0:T(8,128)(2,1)S(1)}, bf16[1024,512]{1,0:T(8,128)(2,1)}, u32[]{:S(2)}) copy-start(bf16[1024,512]{1,0:T(8,128)(2,1)} %param.19) | copy-start | bytes 3145732
  6.5 127.1 %copy-start.5 = (bf16[512]{0:T(512)(128)(2,1)S(1)}, bf16[512]{0:T(512)(128)(2,1)}, u32[]{:S(2)}) copy-start(bf16[512]{0:T(512)(128)(2,1)} %param.20) | copy-start | bytes 3076
  6.5 217.5 %copy-start.6 = (f32[256]{0:T(256)S(1)}, f32[256]{0:T(256)}, u32[]{:S(2)}) copy-start(f32[256]{0:T(256)} %param.16) | copy-start | bytes 3076
  6.6 217.6 %copy-start.4 = (s32[256,128]{1,0:T(8,128)S(1)}, s32[256,128]{1,0:T(8,128)}, u32[]{:S(2)}) copy-start(s32[256,128]{1,0:T(8,128)} %param.15) | copy-start | bytes 393220
  6.6 98.2 %reduce-scatter.3.cloned.1.call-start = ((), (), s32[]{:S(2)}) async-start(), calls=%async_computation.2 | async-start | bytes 1392640 | tf_op jit(solution)/shard_map/reduce_scatter | solution.py:63
  24.0 142.5 %reduce-scatter.5.cloned.1.call-start = ((), (), s32[]{:S(2)}) async-start(), calls=%async_computation.3 | async-start | bytes 589824 | tf_op jit(solution)/shard_map/reduce_scatter | solution.py:118
  133.6 148.9 %all-gather.3.cloned.1.call-start = ((), (), s32[]{:S(2)}) async-start(), calls=%async_computation.4 | async-start | bytes 4456448 | tf_op jit(solution)/shard_map/all_gather | solution.py:126
  289.5 16.3 %collective-permute-start = (f32[128,512]{1,0:T(8,128)S(1)}, f32[128,512]{1,0:T(8,128)S(1)}, u32[]{:S(2)}, u32[]{:S(2)}) collective-permute-start(f32[128,512]{1,0:T(8,128)S(1)} %constant_dynamic-slice_fusion.1), channel_id=1, source_target_pairs={{0,128},{128,0},{1,129},{129,1},{2,130},{130,2},{3,131},{131,3},{4... | collective-permute-start | bytes 786440 | tf_op jit(solution)/shard_map/ppermute | solution.py:17
Sparse Core Ops, SparseCore 0:
  24.1 80.6 reduce-scatter.2
  133.7 32.7 reduce-scatter.4
  224.2 58.2 all-gather.2
